TPU v7x, 256 devices: a whole 4x4x8 slice. The times are simulated.
256 devices in a mesh: gx: 64 (over z_lo, x, y), gz: 4 (over z_hi, core).
Axes of the slice: x: 4, y: 4, z: 8 (z_hi: 2, z_lo: 4; z = z_hi * 4 + z_lo), core: 2. Of those that a mesh axis runs over, the one named last changes fastest.
Arguments:
- residual: float32 [1024, 512], P('gx', 'gz'), may hold values from -6 to 6
- whitening: float32 [1024, 512], P('gx', 'gz'), may hold values from 0.3 to 3
- kernel: float32 [256, 289], P('gz'), may hold values from -0.375 to 0.375
- adjoint_end: float32 [256, 1024, 512], P('gz', 'gx'), may hold values from -6 to 6
- pressure: bfloat16 [2, 256, 1024, 512], P(None, 'gz', 'gx'), may hold values from -6 to 6
- log_permeability: float32 [256, 1024, 512], P('gz', 'gx'), may hold values from -0.7 to 0.7
- vertical: bfloat16 [256, 1024, 512], P('gz', 'gx'), may hold values from 8 to 400
- top_layer: int32 [1024, 512], P('gx'), may hold values from 0 to 127
- well_columns: int32 [64], replicated, may hold values from 0 to 524287
Outputs:
- adjoint_start: float32 [256, 1024, 512], P('gz', 'gx')
- gradient: float32 [256, 1024, 512], P('gz', 'gx')
Inputs may be any that keep to these rules, and one draw needn't show every extreme that they name: `well_columns`: indices may repeat.
All inputs are finite; a program needn't handle non-finite values.
Results may differ from a plain program's by a relative error of at most 0.0015.
Values may be sent and summed in bfloat16 or wider, within the bound.
A program may use at most 128 MiB of HBM per device.

v0:
```python
import functools

import jax
import jax.numpy as jnp
from jax import lax
from jax.experimental import pallas as pl
from jax.experimental.pallas import tpu as pltpu
from jax.sharding import PartitionSpec as P

STEP_SIZE = 0.1
HALF = 8
SIDE = 17
FAR = 1e6
MESH = pl.DeviceIdType.MESH
CHUNKS = 4
LANES = 128


def get(ref, at):
    return jnp.concatenate([ref[q, at, :] for q in range(ref.shape[0])], axis=1)


def put(ref, at, value):
    for q in range(ref.shape[0]):
        ref[q, at, :] = value[:, q * LANES : (q + 1) * LANES]


def window_kernel(
    n_gx,
    n_gz,
    depth,
    cols,
    rows,
    residual_ref,
    whitening_ref,
    kernel_ref,
    top_ref,
    wells_ref,
    adjoint_hbm,
    pressure_hbm,
    logk_hbm,
    vertical_hbm,
    out_hbm,
    grad_hbm,
    adj,
    prs,
    mob,
    ver,
    tx,
    ty,
    exp_,
    rec,
    dec,
    mid,
    src,
    gsum,
    fin,
    surf,
    shifted,
    rhs_hi,
    rhs_lo,
    kpad,
    toep,
    tops,
    send_halo,
    recv_halo,
    send_top,
    recv_top,
    send_mid,
    recv_mid,
    send_inc,
    recv_inc,
    load_sem,
    store_sem,
    surf_send,
    surf_recv,
    edge_send,
    edge_recv,
    halo_send,
    halo_recv,
    top_send,
    top_recv,
    mid_send,
    mid_recv,
    inc_send,
    inc_recv,
):
    gx = lax.axis_index("gx")
    gz = lax.axis_index("gz")
    layers = depth // CHUNKS
    span = layers * cols
    has = (gx > 0, gx < n_gx - 1)
    beside = (gx - 1, gx + 1)

    def loads(c):
        at = c * span
        here = pl.ds(at, span)
        there = pl.ds(depth * cols + at, span)
        pairs = [
            (pressure_hbm.at[here], prs.at[here]),
            (pressure_hbm.at[there], prs.at[there]),
        ]
        for q in range(rows // LANES):
            lane = pl.ds(q * LANES, LANES)
            pairs.append((adjoint_hbm.at[here, lane], adj.at[q, here]))
            pairs.append((logk_hbm.at[here, lane], mob.at[q, here]))
        pairs.append((vertical_hbm.at[here], ver.at[here]))
        return [
            pltpu.make_async_copy(a, b, load_sem.at[c, i]) for i, (a, b) in enumerate(pairs)
        ]

    for c in reversed(range(CHUNKS)):
        for copy in loads(c):
            copy.start()

    barrier = pltpu.get_barrier_semaphore()
    for j in range(1, n_gz):
        pl.semaphore_signal(
            barrier, inc=1, device_id=(gx, lax.rem(gz + j, n_gz)), device_id_type=MESH
        )
    for s in range(2):

        @pl.when(has[s])
        def _():
            pl.semaphore_signal(barrier, inc=1, device_id=(beside[s], gz), device_id_type=MESH)

    strip = surf.at[gz]
    strip[HALF : HALF + cols, :] = residual_ref[...] * whitening_ref[...]
    for s in range(2):

        @pl.when(jnp.logical_not(has[s]))
        def _():
            first = s * (HALF + cols)
            surf[:, first : first + HALF, :] = jnp.zeros((n_gz, HALF, rows // n_gz), jnp.float32)
            recv_halo[s] = jnp.zeros(recv_halo.shape[1:], recv_halo.dtype)
            recv_top[s] = jnp.full(recv_top.shape[1:], FAR, jnp.float32)
            recv_mid[s] = jnp.zeros(recv_mid.shape[1:], recv_mid.dtype)

    @pl.when(gz == n_gz - 1)
    def _():
        recv_inc[...] = jnp.zeros(recv_inc.shape, jnp.float32)

    cell = (
        (gx * cols + lax.broadcasted_iota(jnp.int32, (cols, rows), 0)) * rows
        + lax.broadcasted_iota(jnp.int32, (cols, rows), 1)
    )

    def drill(i, top):
        return jnp.where(cell == wells_ref[i], FAR, top)

    top = lax.fori_loop(0, wells_ref.shape[0], drill, top_ref[...].astype(jnp.float32))
    x_id = lax.broadcasted_iota(jnp.int32, (cols, rows), 0)
    y_id = lax.broadcasted_iota(jnp.int32, (cols, rows), 1)
    tops[0] = top
    tops[1] = jnp.where(x_id == cols - 1, FAR, jnp.maximum(top, pltpu.roll(top, cols - 1, 0)))
    tops[2] = jnp.where(y_id == rows - 1, FAR, jnp.maximum(top, pltpu.roll(top, rows - 1, 1)))
    send_top[0] = jnp.broadcast_to(top[0:1, :], (8, rows))
    send_top[1] = jnp.broadcast_to(top[cols - 1 : cols, :], (8, rows))

    kpad[...] = jnp.zeros(kpad.shape, jnp.float32)
    kpad[:, 0 : SIDE * SIDE] = kernel_ref[...]
    for x in range(8):
        put(toep, pl.ds(x, depth, stride=8), pltpu.roll(kpad[...], SIDE * x, 1))
    tail = shifted.shape[1] - (cols + 2 * HALF) * SIDE
    put(shifted, pl.ds((cols + 2 * HALF) * SIDE, tail), jnp.zeros((tail, rows), jnp.float32))

    strips_beside = jnp.where(has[0], 1, 0) + jnp.where(has[1], 1, 0)
    pl.semaphore_wait(barrier, n_gz - 1 + strips_beside)

    def surf_copy(j):
        mine = surf.at[gz, pl.ds(HALF, cols), :]
        return pltpu.make_async_remote_copy(
            src_ref=mine,
            dst_ref=mine,
            send_sem=surf_send.at[j - 1],
            recv_sem=surf_recv.at[j - 1],
            device_id=(gx, lax.rem(gz + j, n_gz)),
            device_id_type=MESH,
        )

    for j in range(1, n_gz):
        surf_copy(j).start()

    def select_rows(side_col):
        z_of = lax.broadcasted_iota(jnp.int32, (16, 256), 0)
        k_of = lax.broadcasted_iota(jnp.int32, (16, 256), 1)
        return (k_of == z_of * cols + side_col).astype(jnp.bfloat16)

    for c in reversed(range(CHUNKS)):
        for copy in loads(c):
            copy.wait()

    def pack(i, carry):
        z0 = pl.multiple_of(i * 16, 16)
        r0 = pl.multiple_of(i * 16 * cols, 16 * cols)
        for s in range(2):
            x = s * (cols - 1)
            line = pl.ds(r0 + x, 16, stride=cols)
            send_halo[s, pl.ds(z0, 16), :] = get(adj, line).astype(jnp.bfloat16)
            send_halo[s, pl.ds(depth + z0, 16), :] = jnp.exp(get(mob, line)).astype(jnp.bfloat16)
            pick = select_rows(x)
            for k in range(2):
                block = prs[pl.ds(k * depth * cols + r0, 16 * cols), :]
                send_halo[s, pl.ds((2 + k) * depth + z0, 16), :] = jnp.dot(
                    pick, block, preferred_element_type=jnp.float32
                ).astype(jnp.bfloat16)
        return carry

    lax.fori_loop(0, depth // 16, pack, 0)

    def side_copies(s):
        out = []
        for a, b, ss, rs in (
            (send_top, recv_top, top_send, top_recv),
            (send_halo, recv_halo, halo_send, halo_recv),
        ):
            out.append(
                pltpu.make_async_remote_copy(
                    src_ref=a.at[s],
                    dst_ref=b.at[1 - s],
                    send_sem=ss.at[s],
                    recv_sem=rs.at[1 - s],
                    device_id=(beside[s], gz),
                    device_id_type=MESH,
                )
            )
        return out

    def side_arrivals(s):
        return [
            pltpu.make_async_remote_copy(
                src_ref=a.at[1 - s],
                dst_ref=b.at[s],
                send_sem=ss.at[1 - s],
                recv_sem=rs.at[s],
                device_id=(beside[s], gz),
                device_id_type=MESH,
            )
            for a, b, ss, rs in (
                (send_top, recv_top, top_send, top_recv),
                (send_halo, recv_halo, halo_send, halo_recv),
            )
        ]

    for s in range(2):

        @pl.when(has[s])
        def _():
            for copy in side_copies(s):
                copy.start()

    z_base = gz * depth

    def faces(value, back):
        return value - pltpu.roll(value, back, 0)

    def lateral(z, a, p, tface_x, tface_y, zf):
        dx = jnp.where(tops[1] <= zf, pltpu.roll(a, cols - 1, 0) - a, 0.0)
        gxx = dx * (pltpu.roll(p, cols - 1, 0) - p)
        fx = tface_x * dx
        dy = jnp.where(tops[2] <= zf, pltpu.roll(a, rows - 1, 1) - a, 0.0)
        gyy = dy * (pltpu.roll(p, rows - 1, 1) - p)
        fy = tface_y * dy
        flux = (fx - pltpu.roll(fx, 1, 0)) + (fy - pltpu.roll(fy, 1, 1))
        term = (gxx + pltpu.roll(gxx, 1, 0)) + (gyy + pltpu.roll(gyy, 1, 1))
        return flux, term

    def first_layer(i, decay):
        z = depth - 1 - i
        here = pl.ds(pl.multiple_of(z * cols, cols), cols)
        zf = (z_base + z).astype(jnp.float32)
        m = jnp.exp(get(mob, here))
        put(mob, here, m)
        half_m = (0.5 * STEP_SIZE) * m
        tface_x = half_m + pltpu.roll(half_m, cols - 1, 0)
        tface_y = half_m + pltpu.roll(half_m, rows - 1, 1)
        tx[here, :] = tface_x
        ty[here, :] = tface_y
        a = get(adj, here)
        flux, term = lateral(z, a, prs[here, :].astype(jnp.float32), tface_x, tface_y, zf)
        put(exp_, here, a + flux)
        put(gsum, here, term)
        r = 1.0 / (1.0 + ver[here, :].astype(jnp.float32))
        rec[here, :] = r
        decay = jnp.where(tops[0] <= zf, decay - r * decay, 0.0)
        put(dec, here, decay)
        return decay

    decay = jnp.ones((cols, rows), jnp.float32)
    decay = lax.fori_loop(0, depth // 2, first_layer, decay)

    def edge_copy(s):
        first = HALF + s * (cols - HALF)
        return pltpu.make_async_remote_copy(
            src_ref=surf.at[:, pl.ds(first, HALF), :],
            dst_ref=surf.at[:, pl.ds((1 - s) * (HALF + cols), HALF), :],
            send_sem=edge_send.at[s],
            recv_sem=edge_recv.at[1 - s],
            device_id=(beside[s], gz),
            device_id_type=MESH,
        )

    def edge_arrival(s):
        first = HALF + (1 - s) * (cols - HALF)
        return pltpu.make_async_remote_copy(
            src_ref=surf.at[:, pl.ds(first, HALF), :],
            dst_ref=surf.at[:, pl.ds(s * (HALF + cols), HALF), :],
            send_sem=edge_send.at[1 - s],
            recv_sem=edge_recv.at[s],
            device_id=(beside[s], gz),
            device_id_type=MESH,
        )

    def surf_arrival(j):
        theirs = surf.at[lax.rem(gz + n_gz - j, n_gz), pl.ds(HALF, cols), :]
        return pltpu.make_async_remote_copy(
            src_ref=theirs,
            dst_ref=theirs,
            send_sem=surf_send.at[j - 1],
            recv_sem=surf_recv.at[j - 1],
            device_id=(gx, lax.rem(gz + j, n_gz)),
            device_id_type=MESH,
        )

    for j in range(1, n_gz):
        surf_arrival(j).wait_recv()
    for s in range(2):

        @pl.when(has[s])
        def _():
            edge_copy(s).start()

    lax.fori_loop(depth // 2, depth, first_layer, decay)

    for s in range(2):

        @pl.when(has[s])
        def _():
            edge_arrival(s).wait_recv()

    surface = jnp.concatenate([surf[g] for g in range(n_gz)], axis=1)
    wide_y = lax.broadcasted_iota(jnp.int32, surface.shape, 1)
    for b in range(SIDE):
        off = b - HALF
        turned = surface if off == 0 else pltpu.roll(surface, (-off) % rows, 1)
        if off > 0:
            turned = jnp.where(wide_y < rows - off, turned, 0.0)
        if off < 0:
            turned = jnp.where(wide_y >= -off, turned, 0.0)
        put(shifted, pl.ds(b, cols + 2 * HALF, stride=SIDE), turned)
    for h in range(2):
        for q in range(4):
            piece = get(shifted, pl.ds(h * 8 * SIDE + q * 128, 128))
            hi = piece.astype(jnp.bfloat16)
            rhs_hi[h, pl.ds(q * 128, 128), :] = hi
            rhs_lo[h, pl.ds(q * 128, 128), :] = (piece - hi.astype(jnp.float32)).astype(
                jnp.bfloat16
            )

    def product(i, carry):
        tile = pl.ds(pl.multiple_of(i * 128, 128), 128)
        lhs = get(toep, tile)
        hi = lhs.astype(jnp.bfloat16)
        lo = (lhs - hi.astype(jnp.float32)).astype(jnp.bfloat16)
        for h in range(2):
            src[h, tile, :] = (
                jnp.dot(hi, rhs_hi[h], preferred_element_type=jnp.float32)
                + jnp.dot(hi, rhs_lo[h], preferred_element_type=jnp.float32)
                + jnp.dot(lo, rhs_hi[h], preferred_element_type=jnp.float32)
            )
        return carry

    lax.fori_loop(0, depth * 8 // 128, product, 0)

    for s in range(2):

        @pl.when(has[s])
        def _():
            for copy in side_arrivals(s):
                copy.wait_recv()

    def edges(state, arrived, level):
        def step(i, carry):
            z0 = pl.multiple_of(i * 16, 16)
            r0 = pl.multiple_of(i * 16 * cols, 16 * cols)
            zf = (z_base + z0 + lax.broadcasted_iota(jnp.int32, (16, rows), 0)).astype(jnp.float32)
            for s in range(2):
                x = s * (cols - 1)
                line = pl.ds(r0 + x, 16, stride=cols)
                near = get(state, line)
                far = arrived[s, pl.ds(z0, 16), :].astype(jnp.float32)
                far_m = recv_halo[s, pl.ds(depth + z0, 16), :].astype(jnp.float32)
                far_p = recv_halo[s, pl.ds((2 + level) * depth + z0, 16), :].astype(jnp.float32)
                near_p = send_halo[s, pl.ds((2 + level) * depth + z0, 16), :].astype(jnp.float32)
                face = jnp.maximum(tops[0, x : x + 1, :], recv_top[s, 0:1, :])
                d = jnp.where(face <= zf, far - near, 0.0)
                flux = (0.5 * STEP_SIZE) * (get(mob, line) + far_m) * d
                put(exp_, line, get(exp_, line) + flux)
                put(gsum, line, get(gsum, line) + d * (far_p - near_p))
            return carry

        lax.fori_loop(0, depth // 16, step, 0)

    edges(adj, recv_halo, 0)

    def split(z):
        r = pl.multiple_of(z * cols, cols)
        return [pl.ds(r, 8), pl.ds(pl.multiple_of(r + 8, 8), 8)]

    def chain_first(i, below):
        z = depth - 1 - i
        zf = (z_base + z).astype(jnp.float32)
        eight = pl.ds(pl.multiple_of(z * 8, 8), 8)
        solved = []
        for h, part in enumerate(split(z)):
            e = get(exp_, part) + src[h, eight, :]
            v = jnp.where(
                tops[0, 8 * h : 8 * h + 8, :] <= zf, below[h] + rec[part, :] * (e - below[h]), 0.0
            )
            put(mid, part, v)
            solved.append(v)
        return tuple(solved)

    nothing = (jnp.zeros((8, rows), jnp.float32),) * 2
    lax.fori_loop(0, depth, chain_first, nothing)

    def inc_copy(level):
        return pltpu.make_async_remote_copy(
            src_ref=send_inc.at[level],
            dst_ref=recv_inc.at[level],
            send_sem=inc_send.at[level],
            recv_sem=inc_recv.at[level],
            device_id=(gx, gz - 1),
            device_id_type=MESH,
        )

    def inc_arrival(level):
        return pltpu.make_async_remote_copy(
            src_ref=send_inc.at[level],
            dst_ref=recv_inc.at[level],
            send_sem=inc_send.at[level],
            recv_sem=inc_recv.at[level],
            device_id=(gx, gz + 1),
            device_id_type=MESH,
        )

    def relay(level):
        @pl.when(gz < n_gz - 1)
        def _():
            inc_arrival(level).wait_recv()

        @pl.when(gz > 0)
        def _():
            first = pl.ds(0, cols)
            send_inc[level] = get(mid, first) + get(dec, first) * recv_inc[level]
            inc_copy(level).start()

    relay(0)

    def pack_mid(i, carry):
        z0 = pl.multiple_of(i * 16, 16)
        r0 = pl.multiple_of(i * 16 * cols, 16 * cols)
        for s in range(2):
            x = s * (cols - 1)
            line = pl.ds(r0 + x, 16, stride=cols)
            send_mid[s, pl.ds(z0, 16), :] = (
                get(mid, line) + get(dec, line) * recv_inc[0, x : x + 1, :]
            ).astype(jnp.bfloat16)
        return carry

    lax.fori_loop(0, depth // 16, pack_mid, 0)

    def mid_copy(s):
        return pltpu.make_async_remote_copy(
            src_ref=send_mid.at[s],
            dst_ref=recv_mid.at[1 - s],
            send_sem=mid_send.at[s],
            recv_sem=mid_recv.at[1 - s],
            device_id=(beside[s], gz),
            device_id_type=MESH,
        )

    def mid_arrival(s):
        return pltpu.make_async_remote_copy(
            src_ref=send_mid.at[1 - s],
            dst_ref=recv_mid.at[s],
            send_sem=mid_send.at[1 - s],
            recv_sem=mid_recv.at[s],
            device_id=(beside[s], gz),
            device_id_type=MESH,
        )

    for s in range(2):

        @pl.when(has[s])
        def _():
            mid_copy(s).start()

    def second_layer(i, carry):
        z = depth - 1 - i
        here = pl.ds(pl.multiple_of(z * cols, cols), cols)
        there = pl.ds(pl.multiple_of((depth + z) * cols, cols), cols)
        eight = pl.ds(pl.multiple_of(z * 8, 8), 8)
        zf = (z_base + z).astype(jnp.float32)
        a = get(mid, here) + get(dec, here) * recv_inc[0]
        put(mid, here, a)
        flux, term = lateral(
            z, a, prs[there, :].astype(jnp.float32), tx[here, :], ty[here, :], zf
        )
        source = jnp.concatenate([src[0, eight, :], src[1, eight, :]], axis=0)
        put(exp_, here, a + flux + source)
        put(gsum, here, get(gsum, here) + term)
        return carry

    lax.fori_loop(0, depth, second_layer, 0)

    for s in range(2):

        @pl.when(has[s])
        def _():
            mid_arrival(s).wait_recv()

    edges(mid, recv_mid, 1)

    def chain_second(i, below):
        z = depth - 1 - i
        here = pl.ds(pl.multiple_of(z * cols, cols), cols)
        zf = (z_base + z).astype(jnp.float32)
        v = jnp.where(tops[0] <= zf, below + rec[here, :] * (get(exp_, here) - below), 0.0)
        put(mid, here, v)
        put(gsum, here, (0.5 * STEP_SIZE) * get(mob, here) * get(gsum, here))
        return v

    lax.fori_loop(0, depth, chain_second, jnp.zeros((cols, rows), jnp.float32))

    def grad_copy(q):
        lane = pl.ds(q * LANES, LANES)
        return pltpu.make_async_copy(
            gsum.at[q], grad_hbm.at[:, lane], store_sem.at[CHUNKS + q]
        )

    for q in range(rows // LANES):
        grad_copy(q).start()
    relay(1)

    def finish(i, carry):
        here = pl.ds(pl.multiple_of(i * cols, cols), cols)
        fin[here, :] = get(mid, here) + get(dec, here) * recv_inc[1]
        return carry

    def store(c):
        part = pl.ds(c * span, span)
        return pltpu.make_async_copy(fin.at[part], out_hbm.at[part], store_sem.at[c])

    for c in range(CHUNKS):
        lax.fori_loop(c * layers, (c + 1) * layers, finish, 0)
        store(c).start()

    for j in range(1, n_gz):
        surf_copy(j).wait_send()
    for s in range(2):

        @pl.when(has[s])
        def _():
            for copy in side_copies(s):
                copy.wait_send()
            edge_copy(s).wait_send()
            mid_copy(s).wait_send()

    @pl.when(gz > 0)
    def _():
        inc_copy(0).wait_send()
        inc_copy(1).wait_send()

    for q in range(rows // LANES):
        grad_copy(q).wait()
    for c in range(CHUNKS):
        store(c).wait()


def on_device(
    n_gx,
    n_gz,
    residual,
    whitening,
    kernel,
    adjoint_end,
    pressure,
    log_permeability,
    vertical,
    top_layer,
    well_columns,
):
    depth, cols, rows = adjoint_end.shape
    cells = depth * cols
    f32, b16 = jnp.float32, jnp.bfloat16
    field = pltpu.VMEM((cells, rows), f32)
    lanes = rows // LANES
    banded = pltpu.VMEM((lanes, cells, LANES), f32)
    dma = pltpu.SemaphoreType.DMA
    wide = cols + 2 * HALF
    vmem = pl.BlockSpec(memory_space=pltpu.VMEM)
    smem = pl.BlockSpec(memory_space=pltpu.SMEM)
    hbm = pl.BlockSpec(memory_space=pl.ANY)
    adjoint_start, gradient = pl.pallas_call(
        functools.partial(window_kernel, n_gx, n_gz, depth, cols, rows),
        out_shape=(jax.ShapeDtypeStruct((cells, rows), f32),) * 2,
        in_specs=[vmem, vmem, vmem, vmem, smem, hbm, hbm, hbm, hbm],
        out_specs=(hbm, hbm),
        scratch_shapes=[
            banded,
            pltpu.VMEM((2 * cells, rows), b16),
            banded,
            pltpu.VMEM((cells, rows), b16),
            field,
            field,
            banded,
            field,
            banded,
            banded,
            pltpu.VMEM((2, depth * 8, rows), f32),
            banded,
            field,
            pltpu.VMEM((n_gz, wide, rows // n_gz), f32),
            pltpu.VMEM((lanes, 8 * SIDE + 512, LANES), f32),
            pltpu.VMEM((2, 512, rows), b16),
            pltpu.VMEM((2, 512, rows), b16),
            pltpu.VMEM((depth, 512), f32),
            pltpu.VMEM((4, depth * 8, LANES), f32),
            pltpu.VMEM((3, cols, rows), f32),
            pltpu.VMEM((2, 4 * depth, rows), b16),
            pltpu.VMEM((2, 4 * depth, rows), b16),
            pltpu.VMEM((2, 8, rows), f32),
            pltpu.VMEM((2, 8, rows), f32),
            pltpu.VMEM((2, depth, rows), b16),
            pltpu.VMEM((2, depth, rows), b16),
            pltpu.VMEM((2, cols, rows), f32),
            pltpu.VMEM((2, cols, rows), f32),
            dma((CHUNKS, 3 + 2 * lanes)),
            dma((lanes + CHUNKS,)),
            dma((n_gz - 1,)),
            dma((n_gz - 1,)),
        ]
        + [dma((2,))] * 10,
        compiler_params=pltpu.CompilerParams(
            collective_id=0, has_side_effects=True, vmem_limit_bytes=56 * 1024 * 1024
        ),
    )(
        residual,
        whitening,
        kernel,
        top_layer,
        well_columns,
        adjoint_end.reshape(cells, rows),
        pressure.reshape(2 * cells, rows),
        log_permeability.reshape(cells, rows),
        vertical.reshape(cells, rows),
    )
    shape = (depth, cols, rows)
    return adjoint_start.reshape(shape), gradient.reshape(shape)


def solution(mesh):
    in_specs = (
        P("gx", "gz"),
        P("gx", "gz"),
        P("gz", None),
        P("gz", "gx", None),
        P(None, "gz", "gx", None),
        P("gz", "gx", None),
        P("gz", "gx", None),
        P("gx", None),
        P(),
    )
    out_specs = (P("gz", "gx", None), P("gz", "gx", None))
    return jax.shard_map(
        functools.partial(on_device, mesh.shape["gx"], mesh.shape["gz"]),
        mesh=mesh,
        in_specs=in_specs,
        out_specs=out_specs,
        check_vma=False,
    )
```

profile of v0, /device:TPU:33, one launch (start us, length us, event | category | flops | bytes accessed | tf_op | source)
XLA Modules:
  0.0 52.7 jit_solution(617394164199244598)
XLA Ops:
  0.6 47.4 %shard_map.104 = (f32[1024,512]{1,0:T(8,128)}, f32[1024,512]{1,0:T(8,128)}) custom-call(f32[16,128]{1,0:T(8,128)} %residual_ref.1, f32[16,128]{1,0:T(8,128)} %whitening_ref.1, f32[64,289]{1,0:T(8,128)} %kernel_ref.1, s32[16,512]{1,0:T(8,128)} %top_ref.1, s32[64]{0:T(128)} %wells_ref.1, f32[1024,512]{1,0:T(8,128)} %bitcast.8, bf16[2048,512]{1,0:T(8,128)(2,1)} %bitcast.9, ...), custom_call_target="tpu_custom_call" | custom-call | tf_op jit(solution)/shard_map/pallas_call | solution.py:605
  48.0 0.0 copy-start
  48.0 3.4 %copy.13 = f32[64,16,512]{2,1,0:T(8,128)} copy(f32[64,16,512]{2,1,0:T(8,128)} %bitcast.7) | data formatting | bytes 4194304
  51.4 0.0 copy-done
  51.4 1.3 %copy.14 = f32[64,16,512]{2,1,0:T(8,128)} copy(f32[64,16,512]{2,1,0:T(8,128)S(1)} %bitcast.6) | data formatting | bytes 4194304
Async XLA Ops:
  48.0 3.4 %copy-start = (f32[1024,512]{1,0:T(8,128)S(1)}, f32[1024,512]{1,0:T(8,128)}, u32[]{:S(2)}) copy-start(f32[1024,512]{1,0:T(8,128)} %get-tuple-element.5) | copy-start | bytes 6291460
where the time goes:
time: 53.4 us; the launch traced here: 52.7 us
  Pallas kernels  47.4 us (89%)
  local copies, waits for them, and re-layouts  4.69 us (9%)
  between operations  0.65 us (1%)
    pallas_call x1, Pallas kernels, on_device(): pl.pallas_call(functools.partial(window_kernel, n_gx, n_gz, depth, cols,...  47.4 us
    unnamed x4, local copies, waits for them, and re-layouts  4.69 us

commit v1 on v0

v1 whole, which is shorter than its diff:
```python
import functools

import jax
import jax.numpy as jnp
from jax import lax
from jax.experimental import pallas as pl
from jax.experimental.pallas import tpu as pltpu
from jax.sharding import PartitionSpec as P

STEP_SIZE = 0.1
HALF = 8
SIDE = 17
FAR = 1e6
MESH = pl.DeviceIdType.MESH
CHUNKS = 2
UNROLL = 4
LANES = 128


def get(ref, at):
    return jnp.concatenate([ref[q, at, :] for q in range(ref.shape[0])], axis=1)


def put(ref, at, value):
    for q in range(ref.shape[0]):
        ref[q, at, :] = value[:, q * LANES : (q + 1) * LANES]


def every(low, high, unroll, body):
    def step(i, carry):
        body(i)
        return carry

    lax.fori_loop(low, high, step, 0, unroll=unroll)


def window_kernel(
    n_gx,
    n_gz,
    depth,
    cols,
    rows,
    residual_hbm,
    whitening_hbm,
    kernel_hbm,
    top_hbm,
    wells_hbm,
    adjoint_hbm,
    pressure_hbm,
    logk_hbm,
    vertical_hbm,
    out_ref,
    grad_ref,
    residual_ref,
    whitening_ref,
    kernel_ref,
    top_ref,
    wells_ref,
    adj,
    prs,
    mob,
    ver,
    tx,
    ty,
    fx,
    gx_sum,
    gy_sum,
    part_exp,
    steps_y,
    rec,
    fac,
    dec,
    low,
    mid,
    src,
    surf,
    shifted,
    rhs_hi,
    rhs_lo,
    kpad,
    toep,
    toep_hi,
    toep_lo,
    tops,
    near_adj,
    near_mob,
    edge_flux,
    edge_term,
    send_halo,
    recv_halo,
    send_prs,
    recv_prs,
    send_top,
    recv_top,
    send_mid,
    recv_mid,
    send_inc,
    recv_inc,
    small_sem,
    load_sem,
    surf_send,
    surf_recv,
    edge_send,
    edge_recv,
    halo_send,
    halo_recv,
    prs_send,
    prs_recv,
    top_send,
    top_recv,
    mid_send,
    mid_recv,
    inc_send,
    inc_recv,
):
    gx = lax.axis_index("gx")
    gz = lax.axis_index("gz")
    layers = depth // CHUNKS
    span = layers * cols
    cells = depth * cols
    bands = rows // LANES
    has = (gx > 0, gx < n_gx - 1)
    beside = (gx - 1, gx + 1)

    barrier = pltpu.get_barrier_semaphore()
    for j in range(1, n_gz):
        pl.semaphore_signal(
            barrier, inc=1, device_id=(gx, lax.rem(gz + j, n_gz)), device_id_type=MESH
        )
    for s in range(2):

        @pl.when(has[s])
        def _():
            pl.semaphore_signal(barrier, inc=1, device_id=(beside[s], gz), device_id_type=MESH)

    small = [
        pltpu.make_async_copy(a, b, small_sem.at[i])
        for i, (a, b) in enumerate(
            (
                (residual_hbm, residual_ref),
                (whitening_hbm, whitening_ref),
                (top_hbm, top_ref),
                (wells_hbm, wells_ref),
                (kernel_hbm, kernel_ref),
            )
        )
    ]
    for copy in small:
        copy.start()

    def loads(c):
        at = c * span
        here = pl.ds(at, span)
        pairs = []
        for q in range(bands):
            lane = pl.ds(q * LANES, LANES)
            pairs.append((logk_hbm.at[here, lane], mob.at[q, here]))
            pairs.append((adjoint_hbm.at[here, lane], adj.at[q, here]))
        pairs.append((vertical_hbm.at[here], ver.at[here]))
        return [
            pltpu.make_async_copy(a, b, load_sem.at[c, i]) for i, (a, b) in enumerate(pairs)
        ]

    chunk_loads = [loads(c) for c in range(CHUNKS)]
    for copies in reversed(chunk_loads):
        for copy in copies[: 2 * bands]:
            copy.start()
    for copies in reversed(chunk_loads):
        copies[2 * bands].start()
    load_prs = pltpu.make_async_copy(pressure_hbm, prs, small_sem.at[5])
    load_prs.start()

    for s in range(2):

        @pl.when(jnp.logical_not(has[s]))
        def _():
            first = s * (HALF + cols)
            surf[:, first : first + HALF, :] = jnp.zeros((n_gz, HALF, rows // n_gz), jnp.float32)
            recv_halo[s] = jnp.zeros(recv_halo.shape[1:], recv_halo.dtype)
            recv_top[s] = jnp.full(recv_top.shape[1:], FAR, jnp.float32)
            recv_mid[s] = jnp.zeros(recv_mid.shape[1:], recv_mid.dtype)
            recv_prs[s] = jnp.zeros(recv_prs.shape[1:], recv_prs.dtype)

    @pl.when(gz == n_gz - 1)
    def _():
        recv_inc[...] = jnp.zeros(recv_inc.shape, jnp.float32)

    blank = jnp.zeros((8, rows), jnp.float32)
    after = pl.ds(cells, 8)
    for ref in (mob, adj, low, dec, mid):
        put(ref, after, blank)
    for ref in (fx, gx_sum):
        put(ref, pl.ds(0, 8), blank)

    small[0].wait()
    small[1].wait()
    strip = surf.at[gz]
    strip[HALF : HALF + cols, :] = residual_ref[...] * whitening_ref[...]

    small[2].wait()
    small[3].wait()
    cell = (
        (gx * cols + lax.broadcasted_iota(jnp.int32, (cols, rows), 0)) * rows
        + lax.broadcasted_iota(jnp.int32, (cols, rows), 1)
    )

    def drill(i, top):
        return jnp.where(cell == wells_ref[i], FAR, top)

    top = lax.fori_loop(
        0, wells_ref.shape[0], drill, top_ref[...].astype(jnp.float32), unroll=8
    )
    x_id = lax.broadcasted_iota(jnp.int32, (cols, rows), 0)
    y_id = lax.broadcasted_iota(jnp.int32, (cols, rows), 1)
    tops[0] = top
    tops[1] = jnp.where(x_id == cols - 1, FAR, jnp.maximum(top, pltpu.roll(top, cols - 1, 0)))
    tops[2] = jnp.where(y_id == rows - 1, FAR, jnp.maximum(top, pltpu.roll(top, rows - 1, 1)))
    send_top[0] = jnp.broadcast_to(top[0:1, :], (8, rows))
    send_top[1] = jnp.broadcast_to(top[cols - 1 : cols, :], (8, rows))

    strips_beside = jnp.where(has[0], 1, 0) + jnp.where(has[1], 1, 0)
    pl.semaphore_wait(barrier, n_gz - 1 + strips_beside)

    def surf_copy(j):
        mine = surf.at[gz, pl.ds(HALF, cols), :]
        return pltpu.make_async_remote_copy(
            src_ref=mine,
            dst_ref=mine,
            send_sem=surf_send.at[j - 1],
            recv_sem=surf_recv.at[j - 1],
            device_id=(gx, lax.rem(gz + j, n_gz)),
            device_id_type=MESH,
        )

    def surf_arrival(j):
        theirs = surf.at[lax.rem(gz + n_gz - j, n_gz), pl.ds(HALF, cols), :]
        return pltpu.make_async_remote_copy(
            src_ref=theirs,
            dst_ref=theirs,
            send_sem=surf_send.at[j - 1],
            recv_sem=surf_recv.at[j - 1],
            device_id=(gx, lax.rem(gz + j, n_gz)),
            device_id_type=MESH,
        )

    for j in range(1, n_gz):
        surf_copy(j).start()

    for c in range(CHUNKS):
        for copy in chunk_loads[c][: 2 * bands]:
            copy.wait()

    def mobility(logk):
        return (0.5 * STEP_SIZE) * jnp.exp(logk)

    def pack(i):
        z0 = pl.multiple_of(i * 16, 16)
        r0 = pl.multiple_of(i * 16 * cols, 16 * cols)
        for s in range(2):
            line = pl.ds(r0 + s * (cols - 1), 16, stride=cols)
            fields = (get(adj, line), mobility(get(mob, line)))
            near_adj[0, s, pl.ds(z0, 16), :] = fields[0]
            near_mob[s, pl.ds(z0, 16), :] = fields[1]
            for k, field in enumerate(fields):
                send_halo[s, pl.ds(k * depth + z0, 16), :] = field.astype(jnp.bfloat16)

    every(0, depth // 16, 1, pack)

    def swap(sent, arrived, send_sem, recv_sem):
        def leave(s):
            return pltpu.make_async_remote_copy(
                src_ref=sent.at[s],
                dst_ref=arrived.at[1 - s],
                send_sem=send_sem.at[s],
                recv_sem=recv_sem.at[1 - s],
                device_id=(beside[s], gz),
                device_id_type=MESH,
            )

        def come(s):
            return pltpu.make_async_remote_copy(
                src_ref=sent.at[1 - s],
                dst_ref=arrived.at[s],
                send_sem=send_sem.at[1 - s],
                recv_sem=recv_sem.at[s],
                device_id=(beside[s], gz),
                device_id_type=MESH,
            )

        return leave, come

    top_leave, top_come = swap(send_top, recv_top, top_send, top_recv)
    halo_leave, halo_come = swap(send_halo, recv_halo, halo_send, halo_recv)
    prs_leave, prs_come = swap(send_prs, recv_prs, prs_send, prs_recv)
    mid_leave, mid_come = swap(send_mid, recv_mid, mid_send, mid_recv)

    for s in range(2):

        @pl.when(has[s])
        def _():
            top_leave(s).start()
            halo_leave(s).start()

    small[4].wait()
    kpad[...] = jnp.zeros(kpad.shape, jnp.float32)
    kpad[:, 0 : SIDE * SIDE] = kernel_ref[...]
    for x in range(8):
        put(toep, pl.ds(x, depth, stride=8), pltpu.roll(kpad[...], SIDE * x, 1))
    tail = shifted.shape[1] - (cols + 2 * HALF) * SIDE
    put(shifted, pl.ds((cols + 2 * HALF) * SIDE, tail), jnp.zeros((tail, rows), jnp.float32))

    def halve(i):
        tile = pl.ds(pl.multiple_of(i * 64, 64), 64)
        piece = get(toep, tile)
        hi = piece.astype(jnp.bfloat16)
        toep_hi[tile, :] = hi
        toep_lo[tile, :] = (piece - hi.astype(jnp.float32)).astype(jnp.bfloat16)

    every(0, depth * 8 // 64, 1, halve)

    z_base = gz * depth

    def next_x(ref, at):
        return get(ref, pl.ds(at + 1, cols))

    def next_y(value):
        return pltpu.roll(value, rows - 1, 1)

    def narrow_roll(value, by):
        return pltpu.roll(value.astype(jnp.bfloat16), by, 1).astype(jnp.float32)

    def lower(at):
        return pl.ds(pl.multiple_of(at + 8, 8), cols)

    def lateral(level, a, a_next, at, face_x, face_y):
        put(fx, lower(at), face_x * (a_next - a))
        dy = next_y(a) - a
        steps_y[level, pl.ds(at, cols), :] = dy
        fy = face_y * dy
        part_exp[pl.ds(at, cols), :] = a + (fy - narrow_roll(fy, 1))

    def level_first(i, decay):
        z = depth - 1 - i
        at = pl.multiple_of(z * cols, cols)
        here = pl.ds(at, cols)
        zf = (z_base + z).astype(jnp.float32)
        m = mobility(get(mob, here))
        face_x = jnp.where(tops[1] <= zf, m + mobility(next_x(mob, at)), 0.0)
        face_y = jnp.where(tops[2] <= zf, m + narrow_roll(m, rows - 1), 0.0)
        tx[here, :] = face_x
        ty[here, :] = face_y
        lateral(0, get(adj, here), next_x(adj, at), at, face_x, face_y)
        r = 1.0 / (1.0 + ver[here, :].astype(jnp.float32))
        live = tops[0] <= zf
        rec[here, :] = jnp.where(live, r, 0.0)
        f = jnp.where(live, 1.0 - r, 0.0)
        fac[here, :] = f
        decay = f * decay
        put(dec, here, decay)
        return decay

    decay = jnp.ones((cols, rows), jnp.float32)
    for c in range(CHUNKS):
        chunk_loads[c][2 * bands].wait()
    decay = lax.fori_loop(0, depth // 2, level_first, decay, unroll=UNROLL)

    def edge_copy(s):
        first = HALF + s * (cols - HALF)
        return pltpu.make_async_remote_copy(
            src_ref=surf.at[:, pl.ds(first, HALF), :],
            dst_ref=surf.at[:, pl.ds((1 - s) * (HALF + cols), HALF), :],
            send_sem=edge_send.at[s],
            recv_sem=edge_recv.at[1 - s],
            device_id=(beside[s], gz),
            device_id_type=MESH,
        )

    def edge_arrival(s):
        first = HALF + (1 - s) * (cols - HALF)
        return pltpu.make_async_remote_copy(
            src_ref=surf.at[:, pl.ds(first, HALF), :],
            dst_ref=surf.at[:, pl.ds(s * (HALF + cols), HALF), :],
            send_sem=edge_send.at[1 - s],
            recv_sem=edge_recv.at[s],
            device_id=(beside[s], gz),
            device_id_type=MESH,
        )

    for j in range(1, n_gz):
        surf_arrival(j).wait_recv()
    for s in range(2):

        @pl.when(has[s])
        def _():
            edge_copy(s).start()

    lax.fori_loop(depth // 2, depth, level_first, decay, unroll=UNROLL)

    def side_steps(level, s, i):
        z0 = pl.multiple_of(i * 16, 16)
        part = pl.ds(z0, 16)
        x = s * (cols - 1)
        zf = (z_base + z0 + lax.broadcasted_iota(jnp.int32, (16, rows), 0)).astype(jnp.float32)
        far = (recv_halo if level == 0 else recv_mid)[s, part, :].astype(jnp.float32)
        face = jnp.maximum(tops[0, x : x + 1, :], recv_top[s, 0:1, :])
        return part, jnp.where(face <= zf, far - near_adj[level, s, part, :], 0.0)

    def edges(level):
        def step(i):
            for s in range(2):
                part, d = side_steps(level, s, i)
                far_m = recv_halo[s, pl.ds(pl.multiple_of(depth + i * 16, 16), 16), :]
                put(edge_flux.at[s], part, (near_mob[s, part, :] + far_m.astype(jnp.float32)) * d)

        every(0, depth // 16, 1, step)

    def edge_terms():
        def step(i):
            for s in range(2):
                total = None
                for level in range(2):
                    part, d = side_steps(level, s, i)
                    p_part = pl.ds(pl.multiple_of(level * depth + i * 16, 16), 16)
                    far_p = recv_prs[s, p_part, :].astype(jnp.float32)
                    term = d * (far_p - send_prs[s, p_part, :].astype(jnp.float32))
                    total = term if total is None else total + term
                put(edge_term.at[s], part, total)

        every(0, depth // 16, 1, step)

    def face_terms(level, add):
        state = (adj, mid)[level]

        def step(z):
            at = pl.multiple_of(z * cols, cols)
            here = pl.ds(at, cols)
            zf = (z_base + z).astype(jnp.float32)
            p = prs[pl.ds(pl.multiple_of(level * cells + at, cols), cols), :].astype(jnp.float32)
            a = get(state, here)
            dx = jnp.where(tops[1] <= zf, next_x(state, at) - a, 0.0)
            dy = jnp.where(tops[2] <= zf, steps_y[level, here, :], 0.0)
            term_x = dx * (pltpu.roll(p, cols - 1, 0) - p)
            term_y = dy * (next_y(p) - p)
            if add:
                term_x = term_x + get(gx_sum, lower(at))
                term_y = term_y + gy_sum[here, :]
            put(gx_sum, lower(at), term_x)
            gy_sum[here, :] = term_y

        every(0, depth, UNROLL, step)

    def send_pressures():
        z_of = lax.broadcasted_iota(jnp.int32, (32, 256), 0)
        k_of = lax.broadcasted_iota(jnp.int32, (32, 256), 1)
        pick = (k_of == jnp.where(z_of < 16, z_of * cols, z_of * cols - 15 * cols - 1)).astype(
            jnp.bfloat16
        )

        def step(i):
            block = prs[pl.ds(pl.multiple_of(i * 256, 256), 256), :]
            lines = jnp.dot(pick, block, preferred_element_type=jnp.float32).astype(jnp.bfloat16)
            part = pl.ds(pl.multiple_of(i * 16, 16), 16)
            send_prs[0, part, :] = lines[:16, :]
            send_prs[1, part, :] = lines[16:, :]

        every(0, 2 * depth // 16, 1, step)
        for s in range(2):

            @pl.when(has[s])
            def _():
                prs_leave(s).start()

    for s in range(2):

        @pl.when(has[s])
        def _():
            edge_arrival(s).wait_recv()

    surface = jnp.concatenate([surf[g] for g in range(n_gz)], axis=1)
    wide_y = lax.broadcasted_iota(jnp.int32, surface.shape, 1)
    for b in range(SIDE):
        off = b - HALF
        turned = surface if off == 0 else pltpu.roll(surface, (-off) % rows, 1)
        if off > 0:
            turned = jnp.where(wide_y < rows - off, turned, 0.0)
        if off < 0:
            turned = jnp.where(wide_y >= -off, turned, 0.0)
        put(shifted, pl.ds(b, cols + 2 * HALF, stride=SIDE), turned)
    for h in range(2):
        for q in range(4):
            piece = get(shifted, pl.ds(h * 8 * SIDE + q * 128, 128))
            hi = piece.astype(jnp.bfloat16)
            rhs_hi[h, pl.ds(q * 128, 128), :] = hi
            rhs_lo[h, pl.ds(q * 128, 128), :] = (piece - hi.astype(jnp.float32)).astype(
                jnp.bfloat16
            )

    def product(i):
        tile = pl.ds(pl.multiple_of(i * 256, 256), 256)
        for h in range(2):
            src[h, tile, :] = (
                jnp.dot(toep_hi[tile, :], rhs_hi[h], preferred_element_type=jnp.float32)
                + jnp.dot(toep_hi[tile, :], rhs_lo[h], preferred_element_type=jnp.float32)
                + jnp.dot(toep_lo[tile, :], rhs_hi[h], preferred_element_type=jnp.float32)
            )

    every(0, depth * 8 // 256, 1, product)

    row_id = lax.broadcasted_iota(jnp.int32, (8, rows), 0)

    def edge_rows(ref, z, h):
        line = get(ref.at[h], pl.ds(z, 1))
        return jnp.where(row_id == 7 * h, line, 0.0)

    def chain(i, below):
        z = depth - 1 - i
        eight = pl.ds(pl.multiple_of(z * 8, 8), 8)
        solved = []
        for h in range(2):
            at = pl.multiple_of(z * cols + 8 * h, 8)
            part = pl.ds(at, 8)
            across = get(fx, pl.ds(pl.multiple_of(at + 8, 8), 8)) - get(fx, pl.ds(at + 7, 8))
            e = (part_exp[part, :] + across) + (src[h, eight, :] + edge_rows(edge_flux, z, h))
            v = fac[part, :] * below[h] + rec[part, :] * e
            put(low, part, v)
            solved.append(v)
        return tuple(solved)

    for s in range(2):

        @pl.when(has[s])
        def _():
            top_come(s).wait_recv()
            halo_come(s).wait_recv()

    edges(0)
    nothing = (jnp.zeros((8, rows), jnp.float32),) * 2
    lax.fori_loop(0, depth, chain, nothing, unroll=4)

    def inc_copy(level, to):
        return pltpu.make_async_remote_copy(
            src_ref=send_inc.at[level],
            dst_ref=recv_inc.at[level],
            send_sem=inc_send.at[level],
            recv_sem=inc_recv.at[level],
            device_id=(gx, to),
            device_id_type=MESH,
        )

    def relay(level):
        @pl.when(gz < n_gz - 1)
        def _():
            inc_copy(level, gz + 1).wait_recv()

        @pl.when(gz > 0)
        def _():
            first = pl.ds(0, cols)
            send_inc[level] = get(low, first) + get(dec, first) * recv_inc[level]
            inc_copy(level, gz - 1).start()

    load_prs.wait()
    early = gz < n_gz // 2

    @pl.when(early)
    def _():
        send_pressures()
        face_terms(0, False)

    relay(0)

    def pack_mid(i):
        z0 = pl.multiple_of(i * 16, 16)
        r0 = pl.multiple_of(i * 16 * cols, 16 * cols)
        for s in range(2):
            x = s * (cols - 1)
            line = pl.ds(r0 + x, 16, stride=cols)
            value = get(low, line) + get(dec, line) * recv_inc[0, x : x + 1, :]
            near_adj[1, s, pl.ds(z0, 16), :] = value
            send_mid[s, pl.ds(z0, 16), :] = value.astype(jnp.bfloat16)

    every(0, depth // 16, 2, pack_mid)

    for s in range(2):

        @pl.when(has[s])
        def _():
            mid_leave(s).start()

    below_next = pltpu.roll(recv_inc[0], cols - 1, 0)

    def level_second(z):
        at = pl.multiple_of(z * cols, cols)
        here = pl.ds(at, cols)
        a = get(low, here) + get(dec, here) * recv_inc[0]
        a_next = next_x(low, at) + next_x(dec, at) * below_next
        put(mid, here, a)
        lateral(1, a, a_next, at, tx[here, :], ty[here, :])

    every(0, depth, UNROLL, level_second)

    @pl.when(early)
    def _():
        face_terms(1, True)

    @pl.when(jnp.logical_not(early))
    def _():
        send_pressures()
        face_terms(1, False)

    for s in range(2):

        @pl.when(has[s])
        def _():
            mid_come(s).wait_recv()

    edges(1)
    lax.fori_loop(0, depth, chain, nothing, unroll=4)
    relay(1)

    @pl.when(jnp.logical_not(early))
    def _():
        face_terms(0, True)

    for s in range(2):

        @pl.when(has[s])
        def _():
            prs_come(s).wait_recv()

    edge_terms()

    def finish(z):
        at = pl.multiple_of(z * cols, cols)
        here = pl.ds(at, cols)
        out_ref[here, :] = get(low, here) + get(dec, here) * recv_inc[1]
        along = gy_sum[here, :]
        along = along + pltpu.roll(along, 1, 1)
        across = get(gx_sum, lower(at)) + get(gx_sum, pl.ds(at + 7, cols))
        ends = jnp.concatenate([edge_rows(edge_term, z, h) for h in range(2)], axis=0)
        grad_ref[here, :] = mobility(get(mob, here)) * ((along + across) + ends)

    every(0, depth, 4, finish)

    for j in range(1, n_gz):
        surf_copy(j).wait_send()
    for s in range(2):

        @pl.when(has[s])
        def _():
            top_leave(s).wait_send()
            halo_leave(s).wait_send()
            prs_leave(s).wait_send()
            edge_copy(s).wait_send()
            mid_leave(s).wait_send()

    @pl.when(gz > 0)
    def _():
        inc_copy(0, gz - 1).wait_send()
        inc_copy(1, gz - 1).wait_send()


def on_device(
    n_gx,
    n_gz,
    residual,
    whitening,
    kernel,
    adjoint_end,
    pressure,
    log_permeability,
    vertical,
    top_layer,
    well_columns,
):
    depth, cols, rows = adjoint_end.shape
    cells = depth * cols
    f32, b16 = jnp.float32, jnp.bfloat16
    lanes = rows // LANES
    vmem = pltpu.VMEM
    field = vmem((cells, rows), f32)
    banded = vmem((lanes, cells + 8, LANES), f32)
    dma = pltpu.SemaphoreType.DMA
    wide = cols + 2 * HALF
    hbm = pl.BlockSpec(memory_space=pl.ANY)
    adjoint_start, gradient = pl.pallas_call(
        functools.partial(window_kernel, n_gx, n_gz, depth, cols, rows),
        out_shape=(vmem((cells, rows), f32),) * 2,
        in_specs=[hbm] * 9,
        out_specs=(pl.BlockSpec(memory_space=vmem),) * 2,
        scratch_shapes=[
            vmem(residual.shape, f32),
            vmem(whitening.shape, f32),
            vmem(kernel.shape, f32),
            vmem(top_layer.shape, jnp.int32),
            pltpu.SMEM(well_columns.shape, jnp.int32),
            banded,
            vmem((2 * cells, rows), b16),
            banded,
            vmem((cells, rows), b16),
            field,
            field,
            banded,
            banded,
            field,
            field,
            vmem((2, cells, rows), f32),
            field,
            field,
            banded,
            banded,
            banded,
            vmem((2, depth * 8, rows), f32),
            vmem((n_gz, wide, rows // n_gz), f32),
            vmem((lanes, 8 * SIDE + 512, LANES), f32),
            vmem((2, 512, rows), b16),
            vmem((2, 512, rows), b16),
            vmem((depth, 512), f32),
            vmem((4, depth * 8, LANES), f32),
            vmem((depth * 8, 512), b16),
            vmem((depth * 8, 512), b16),
            vmem((3, cols, rows), f32),
            vmem((2, 2, depth, rows), f32),
            vmem((2, depth, rows), f32),
            vmem((2, lanes, depth, LANES), f32),
            vmem((2, lanes, depth, LANES), f32),
            vmem((2, 2 * depth, rows), b16),
            vmem((2, 2 * depth, rows), b16),
            vmem((2, 2 * depth, rows), b16),
            vmem((2, 2 * depth, rows), b16),
            vmem((2, 8, rows), f32),
            vmem((2, 8, rows), f32),
            vmem((2, depth, rows), b16),
            vmem((2, depth, rows), b16),
            vmem((2, cols, rows), f32),
            vmem((2, cols, rows), f32),
            dma((6,)),
            dma((CHUNKS, 1 + 2 * lanes)),
            dma((n_gz - 1,)),
            dma((n_gz - 1,)),
        ]
        + [dma((2,))] * 12,
        compiler_params=pltpu.CompilerParams(
            collective_id=0, has_side_effects=True, vmem_limit_bytes=56 * 1024 * 1024
        ),
    )(
        residual,
        whitening,
        kernel,
        top_layer,
        well_columns,
        adjoint_end.reshape(cells, rows),
        pressure.reshape(2 * cells, rows),
        log_permeability.reshape(cells, rows),
        vertical.reshape(cells, rows),
    )
    shape = (depth, cols, rows)
    return adjoint_start.reshape(shape), gradient.reshape(shape)


def solution(mesh):
    in_specs = (
        P("gx", "gz"),
        P("gx", "gz"),
        P("gz", None),
        P("gz", "gx", None),
        P(None, "gz", "gx", None),
        P("gz", "gx", None),
        P("gz", "gx", None),
        P("gx", None),
        P(),
    )
    out_specs = (P("gz", "gx", None), P("gz", "gx", None))
    return jax.shard_map(
        functools.partial(on_device, mesh.shape["gx"], mesh.shape["gz"]),
        mesh=mesh,
        in_specs=in_specs,
        out_specs=out_specs,
        check_vma=False,
    )
```

time: 53.4 us -> 41 us (0.77)
  Pallas kernels: 47.4 us -> 37.1 us
  local copies, waits for them, and re-layouts: 4.69 us -> 2.64 us
    pallas_call x1, Pallas kernels: 47.4 us -> 37.1 us  [on_device(): pl.pallas_call(functools.partial(window_kernel, n_gx, n_gz, depth, cols,...]
    unnamed x4 -> x2, local copies, waits for them, and re-layouts: 4.69 us -> 2.64 us
where the time goes in v1:
time: 41 us; the launch traced here: 40.4 us
  Pallas kernels  37.1 us (90%)
  local copies, waits for them, and re-layouts  2.64 us (6%)
  between operations  0.64 us (2%)
    pallas_call x1, Pallas kernels, on_device(): pl.pallas_call(functools.partial(window_kernel, n_gx, n_gz, depth, cols,...  37.1 us
    unnamed x2, local copies, waits for them, and re-layouts  2.64 us

profile of v1, /device:TPU:33, one launch (start us, length us, event | category | flops | bytes accessed | tf_op | source)
XLA Modules:
  0.0 40.4 jit_solution(10906282457144691215)
XLA Ops:
  0.6 37.1 %shard_map.104 = (f32[1024,512]{1,0:T(8,128)S(1)}, f32[1024,512]{1,0:T(8,128)S(1)}) custom-call(f32[16,128]{1,0:T(8,128)} %residual_hbm.1, f32[16,128]{1,0:T(8,128)} %whitening_hbm.1, f32[64,289]{1,0:T(8,128)} %kernel_hbm.1, s32[16,512]{1,0:T(8,128)} %top_hbm.1, s32[64]{0:T(128)} %wells_hbm.1, f32[1024,512]{1,0:T(8,128)} %bitcast.8, ...), custom_call_target="tpu_custom_call" | custom-call | tf_op jit(solution)/shard_map/pallas_call | solution.py:685
  37.7 1.3 %copy.13 = f32[64,16,512]{2,1,0:T(8,128)} copy(f32[64,16,512]{2,1,0:T(8,128)S(1)} %bitcast.7) | data formatting | bytes 4194304
  39.1 1.3 %copy.14 = f32[64,16,512]{2,1,0:T(8,128)} copy(f32[64,16,512]{2,1,0:T(8,128)S(1)} %bitcast.6) | data formatting | bytes 4194304

commit v2 on v1

--- a/solution.py
+++ b/solution.py
@@ -14,6 +14,8 @@
 MESH = pl.DeviceIdType.MESH
 CHUNKS = 2
 UNROLL = 4
+STORES = 4
+SPLIT = 48
 LANES = 128
 
 
@@ -32,6 +34,62 @@
         return carry
 
     lax.fori_loop(low, high, step, 0, unroll=unroll)
+
+
+def edge_rows(ref, z, h, rows):
+    row_id = lax.broadcasted_iota(jnp.int32, (8, rows), 0)
+    return jnp.where(row_id == 7 * h, get(ref.at[h], pl.ds(z, 1)), 0.0)
+
+
+def finish_kernel(
+    n_gx,
+    depth,
+    cols,
+    rows,
+    low,
+    dec,
+    inc_ref,
+    gx_sum,
+    gy_sum,
+    mob,
+    edge_term,
+    top_ref,
+    out_hbm,
+    grad_hbm,
+    out,
+    grad,
+    sem,
+):
+    z_base = lax.axis_index("gz") * depth
+    chunk = depth // STORES
+
+    def finish(z):
+        at = pl.multiple_of(z * cols, cols)
+        here = pl.ds(at, cols)
+        live = top_ref[...] <= (z_base + z).astype(jnp.float32)
+        out[here, :] = jnp.where(live, get(low, here) + get(dec, here) * inc_ref[...], 0.0)
+        across = get(gx_sum, pl.ds(pl.multiple_of(at + 8, 8), cols)) + get(
+            gx_sum, pl.ds(at + 7, cols)
+        )
+        ends = jnp.concatenate([edge_rows(edge_term, z, h, rows) for h in range(2)], axis=0)
+        grad[here, :] = get(mob, here) * ((gy_sum[here, :] + across) + ends)
+
+    def stores(c):
+        part = pl.ds(c * chunk * cols, chunk * cols)
+        return [
+            pltpu.make_async_copy(a.at[part], b.at[part], sem.at[c, i])
+            for i, (a, b) in enumerate(((out, out_hbm), (grad, grad_hbm)))
+        ]
+
+    pending = []
+    for c in range(STORES):
+        every(c * chunk, (c + 1) * chunk, 4, finish)
+        copies = stores(c)
+        for copy in copies:
+            copy.start()
+        pending += copies
+    for copy in pending:
+        copy.wait()
 
 
 def window_kernel(
@@ -49,8 +107,14 @@
     pressure_hbm,
     logk_hbm,
     vertical_hbm,
-    out_ref,
-    grad_ref,
+    low,
+    dec,
+    inc_ref,
+    gx_sum,
+    gy_sum,
+    mob,
+    edge_term,
+    top_out,
     residual_ref,
     whitening_ref,
     kernel_ref,
@@ -58,19 +122,20 @@
     wells_ref,
     adj,
     prs,
-    mob,
+    logk,
     ver,
     tx,
     ty,
+    face_y,
     fx,
-    gx_sum,
-    gy_sum,
-    part_exp,
+    fy_narrow,
+    flux_y,
     steps_y,
+    gx_part,
+    gy_part,
+    step_x,
+    step_y,
     rec,
-    fac,
-    dec,
-    low,
     mid,
     src,
     surf,
@@ -85,7 +150,8 @@
     near_adj,
     near_mob,
     edge_flux,
-    edge_term,
+    pair_sum,
+    pair_step,
     send_halo,
     recv_halo,
     send_prs,
@@ -154,7 +220,7 @@
         pairs = []
         for q in range(bands):
             lane = pl.ds(q * LANES, LANES)
-            pairs.append((logk_hbm.at[here, lane], mob.at[q, here]))
+            pairs.append((logk_hbm.at[here, lane], logk.at[q, here]))
             pairs.append((adjoint_hbm.at[here, lane], adj.at[q, here]))
         pairs.append((vertical_hbm.at[here], ver.at[here]))
         return [
@@ -187,9 +253,9 @@
 
     blank = jnp.zeros((8, rows), jnp.float32)
     after = pl.ds(cells, 8)
-    for ref in (mob, adj, low, dec, mid):
+    for ref in (mob, adj, low, dec, mid, logk):
         put(ref, after, blank)
-    for ref in (fx, gx_sum):
+    for ref in (fx, gx_sum, gx_part):
         put(ref, pl.ds(0, 8), blank)
 
     small[0].wait()
@@ -213,10 +279,36 @@
     x_id = lax.broadcasted_iota(jnp.int32, (cols, rows), 0)
     y_id = lax.broadcasted_iota(jnp.int32, (cols, rows), 1)
     tops[0] = top
+    top_out[...] = top
     tops[1] = jnp.where(x_id == cols - 1, FAR, jnp.maximum(top, pltpu.roll(top, cols - 1, 0)))
     tops[2] = jnp.where(y_id == rows - 1, FAR, jnp.maximum(top, pltpu.roll(top, rows - 1, 1)))
     send_top[0] = jnp.broadcast_to(top[0:1, :], (8, rows))
     send_top[1] = jnp.broadcast_to(top[cols - 1 : cols, :], (8, rows))
+
+    small[4].wait()
+    kpad[...] = jnp.zeros(kpad.shape, jnp.float32)
+    kpad[:, 0 : SIDE * SIDE] = kernel_ref[...]
+    for x in range(8):
+        put(toep, pl.ds(x, depth, stride=8), pltpu.roll(kpad[...], SIDE * x, 1))
+    tail = shifted.shape[1] - (cols + 2 * HALF) * SIDE
+    put(shifted, pl.ds((cols + 2 * HALF) * SIDE, tail), jnp.zeros((tail, rows), jnp.float32))
+
+    def halve(i):
+        tile = pl.ds(pl.multiple_of(i * 64, 64), 64)
+        piece = get(toep, tile)
+        hi = piece.astype(jnp.bfloat16)
+        toep_hi[tile, :] = hi
+        toep_lo[tile, :] = (piece - hi.astype(jnp.float32)).astype(jnp.bfloat16)
+
+    every(0, depth * 8 // 64, 1, halve)
+
+    tile = rows // 2
+    k_id = lax.broadcasted_iota(jnp.int32, (rows, tile), 0)
+    n_id = lax.broadcasted_iota(jnp.int32, (rows, tile), 1)
+    same, nearby = k_id == n_id, k_id == n_id + 1
+    pair_sum[...] = jnp.where(same, 1.0, jnp.where(nearby, 1.0, 0.0)).astype(jnp.bfloat16)
+    same, nearby = k_id == n_id + tile, k_id + 1 == n_id + tile
+    pair_step[...] = jnp.where(same, 1.0, jnp.where(nearby, -1.0, 0.0)).astype(jnp.bfloat16)
 
     strips_beside = jnp.where(has[0], 1, 0) + jnp.where(has[1], 1, 0)
     pl.semaphore_wait(barrier, n_gz - 1 + strips_beside)
@@ -246,19 +338,36 @@
     for j in range(1, n_gz):
         surf_copy(j).start()
 
-    for c in range(CHUNKS):
+    block = 16 * cols
+
+    def product_of(lhs, rhs):
+        return jnp.dot(lhs, rhs, preferred_element_type=jnp.float32)
+
+    def mobilities(i):
+        at = pl.ds(pl.multiple_of(i * block, block), block)
+        m = (0.5 * STEP_SIZE) * jnp.exp(get(logk, at))
+        put(mob, at, m)
+        m = m.astype(jnp.bfloat16)
+        face_y[at, :tile] = product_of(m, pair_sum[...])
+        face_y[at, tile:] = product_of(m[:, tile:], pair_sum[:tile, :])
+
+    def flux_steps(i):
+        at = pl.ds(pl.multiple_of(i * block, block), block)
+        f = fy_narrow[at, :]
+        flux_y[at, :tile] = product_of(f[:, :tile], pair_step[tile:, :])
+        flux_y[at, tile:] = product_of(f, pair_step[...])
+
+    for c in reversed(range(CHUNKS)):
         for copy in chunk_loads[c][: 2 * bands]:
             copy.wait()
-
-    def mobility(logk):
-        return (0.5 * STEP_SIZE) * jnp.exp(logk)
+        every(c * span // block, (c + 1) * span // block, 2, mobilities)
 
     def pack(i):
         z0 = pl.multiple_of(i * 16, 16)
         r0 = pl.multiple_of(i * 16 * cols, 16 * cols)
         for s in range(2):
             line = pl.ds(r0 + s * (cols - 1), 16, stride=cols)
-            fields = (get(adj, line), mobility(get(mob, line)))
+            fields = (get(adj, line), get(mob, line))
             near_adj[0, s, pl.ds(z0, 16), :] = fields[0]
             near_mob[s, pl.ds(z0, 16), :] = fields[1]
             for k, field in enumerate(fields):
@@ -301,23 +410,6 @@
             top_leave(s).start()
             halo_leave(s).start()
 
-    small[4].wait()
-    kpad[...] = jnp.zeros(kpad.shape, jnp.float32)
-    kpad[:, 0 : SIDE * SIDE] = kernel_ref[...]
-    for x in range(8):
-        put(toep, pl.ds(x, depth, stride=8), pltpu.roll(kpad[...], SIDE * x, 1))
-    tail = shifted.shape[1] - (cols + 2 * HALF) * SIDE
-    put(shifted, pl.ds((cols + 2 * HALF) * SIDE, tail), jnp.zeros((tail, rows), jnp.float32))
-
-    def halve(i):
-        tile = pl.ds(pl.multiple_of(i * 64, 64), 64)
-        piece = get(toep, tile)
-        hi = piece.astype(jnp.bfloat16)
-        toep_hi[tile, :] = hi
-        toep_lo[tile, :] = (piece - hi.astype(jnp.float32)).astype(jnp.bfloat16)
-
-    every(0, depth * 8 // 64, 1, halve)
-
     z_base = gz * depth
 
     def next_x(ref, at):
@@ -326,43 +418,36 @@
     def next_y(value):
         return pltpu.roll(value, rows - 1, 1)
 
-    def narrow_roll(value, by):
-        return pltpu.roll(value.astype(jnp.bfloat16), by, 1).astype(jnp.float32)
-
     def lower(at):
         return pl.ds(pl.multiple_of(at + 8, 8), cols)
 
-    def lateral(level, a, a_next, at, face_x, face_y):
-        put(fx, lower(at), face_x * (a_next - a))
+    def lateral(level, a, a_next, at, open_x, open_y):
+        here = pl.ds(at, cols)
+        put(fx, lower(at), open_x * (a_next - a))
         dy = next_y(a) - a
-        steps_y[level, pl.ds(at, cols), :] = dy
-        fy = face_y * dy
-        part_exp[pl.ds(at, cols), :] = a + (fy - narrow_roll(fy, 1))
+        steps_y[level, here, :] = dy
+        fy_narrow[here, :] = (open_y * dy).astype(jnp.bfloat16)
 
     def level_first(i, decay):
         z = depth - 1 - i
         at = pl.multiple_of(z * cols, cols)
         here = pl.ds(at, cols)
         zf = (z_base + z).astype(jnp.float32)
-        m = mobility(get(mob, here))
-        face_x = jnp.where(tops[1] <= zf, m + mobility(next_x(mob, at)), 0.0)
-        face_y = jnp.where(tops[2] <= zf, m + narrow_roll(m, rows - 1), 0.0)
-        tx[here, :] = face_x
-        ty[here, :] = face_y
-        lateral(0, get(adj, here), next_x(adj, at), at, face_x, face_y)
-        r = 1.0 / (1.0 + ver[here, :].astype(jnp.float32))
-        live = tops[0] <= zf
-        rec[here, :] = jnp.where(live, r, 0.0)
-        f = jnp.where(live, 1.0 - r, 0.0)
-        fac[here, :] = f
-        decay = f * decay
+        open_x = jnp.where(tops[1] <= zf, get(mob, here) + next_x(mob, at), 0.0)
+        open_y = jnp.where(tops[2] <= zf, face_y[here, :], 0.0)
+        tx[here, :] = open_x
+        ty[here, :] = open_y
+        lateral(0, get(adj, here), next_x(adj, at), at, open_x, open_y)
+        r = jnp.where(tops[0] <= zf, 1.0 / (1.0 + ver[here, :].astype(jnp.float32)), 0.0)
+        rec[here, :] = r
+        decay = decay - r * decay
         put(dec, here, decay)
         return decay
 
     decay = jnp.ones((cols, rows), jnp.float32)
     for c in range(CHUNKS):
         chunk_loads[c][2 * bands].wait()
-    decay = lax.fori_loop(0, depth // 2, level_first, decay, unroll=UNROLL)
+    decay = lax.fori_loop(0, SPLIT, level_first, decay, unroll=UNROLL)
 
     def edge_copy(s):
         first = HALF + s * (cols - HALF)
@@ -394,7 +479,8 @@
         def _():
             edge_copy(s).start()
 
-    lax.fori_loop(depth // 2, depth, level_first, decay, unroll=UNROLL)
+    lax.fori_loop(SPLIT, depth, level_first, decay, unroll=UNROLL)
+    every(0, cells // block, 4, flux_steps)
 
     def side_steps(level, s, i):
         z0 = pl.multiple_of(i * 16, 16)
@@ -428,28 +514,41 @@
 
         every(0, depth // 16, 1, step)
 
-    def face_terms(level, add):
+    def pressure_steps(level, z, at):
+        zf = (z_base + z).astype(jnp.float32)
+        p = prs[pl.ds(pl.multiple_of(level * cells + at, cols), cols), :].astype(jnp.float32)
+        across = jnp.where(tops[1] <= zf, pltpu.roll(p, cols - 1, 0) - p, 0.0)
+        return across, jnp.where(tops[2] <= zf, next_y(p) - p, 0.0)
+
+    def prepare_terms(z):
+        at = pl.multiple_of(z * cols, cols)
+        across, along = pressure_steps(1, z, at)
+        step_x[pl.ds(at, cols), :] = across
+        step_y[pl.ds(at, cols), :] = along
+
+    def face_terms(level, add, ready):
         state = (adj, mid)[level]
 
         def step(z):
             at = pl.multiple_of(z * cols, cols)
             here = pl.ds(at, cols)
-            zf = (z_base + z).astype(jnp.float32)
-            p = prs[pl.ds(pl.multiple_of(level * cells + at, cols), cols), :].astype(jnp.float32)
-            a = get(state, here)
-            dx = jnp.where(tops[1] <= zf, next_x(state, at) - a, 0.0)
-            dy = jnp.where(tops[2] <= zf, steps_y[level, here, :], 0.0)
-            term_x = dx * (pltpu.roll(p, cols - 1, 0) - p)
-            term_y = dy * (next_y(p) - p)
+            if ready:
+                across, along = step_x[here, :], step_y[here, :]
+            else:
+                across, along = pressure_steps(level, z, at)
+            term_x = (next_x(state, at) - get(state, here)) * across
+            term_y = steps_y[level, here, :] * along
             if add:
-                term_x = term_x + get(gx_sum, lower(at))
-                term_y = term_y + gy_sum[here, :]
-            put(gx_sum, lower(at), term_x)
-            gy_sum[here, :] = term_y
+                term_x = term_x + get(gx_part, lower(at))
+                term_y = term_y + gy_part[here, :]
+                gy_sum[here, :] = term_y + pltpu.roll(term_y, 1, 1)
+            else:
+                gy_part[here, :] = term_y
+            put(gx_sum if add else gx_part, lower(at), term_x)
 
         every(0, depth, UNROLL, step)
 
-    def send_pressures():
+    def pack_pressures():
         z_of = lax.broadcasted_iota(jnp.int32, (32, 256), 0)
         k_of = lax.broadcasted_iota(jnp.int32, (32, 256), 1)
         pick = (k_of == jnp.where(z_of < 16, z_of * cols, z_of * cols - 15 * cols - 1)).astype(
@@ -464,28 +563,31 @@
             send_prs[1, part, :] = lines[16:, :]
 
         every(0, 2 * depth // 16, 1, step)
-        for s in range(2):
-
-            @pl.when(has[s])
-            def _():
-                prs_leave(s).start()
-
+    load_prs.wait()
+    pack_pressures()
+
+    def shift_rows(first, count):
+        part = jnp.concatenate([surf[g, first : first + count, :] for g in range(n_gz)], axis=1)
+        wide_y = lax.broadcasted_iota(jnp.int32, part.shape, 1)
+        for b in range(SIDE):
+            off = b - HALF
+            turned = part if off == 0 else pltpu.roll(part, (-off) % rows, 1)
+            if off > 0:
+                turned = jnp.where(wide_y < rows - off, turned, 0.0)
+            if off < 0:
+                turned = jnp.where(wide_y >= -off, turned, 0.0)
+            put(shifted, pl.ds(first * SIDE + b, count, stride=SIDE), turned)
+
+    shift_rows(HALF, cols)
     for s in range(2):
 
         @pl.when(has[s])
         def _():
             edge_arrival(s).wait_recv()
-
-    surface = jnp.concatenate([surf[g] for g in range(n_gz)], axis=1)
-    wide_y = lax.broadcasted_iota(jnp.int32, surface.shape, 1)
-    for b in range(SIDE):
-        off = b - HALF
-        turned = surface if off == 0 else pltpu.roll(surface, (-off) % rows, 1)
-        if off > 0:
-            turned = jnp.where(wide_y < rows - off, turned, 0.0)
-        if off < 0:
-            turned = jnp.where(wide_y >= -off, turned, 0.0)
-        put(shifted, pl.ds(b, cols + 2 * HALF, stride=SIDE), turned)
+            prs_leave(s).start()
+
+    for s in range(2):
+        shift_rows(s * (HALF + cols), HALF)
     for h in range(2):
         for q in range(4):
             piece = get(shifted, pl.ds(h * 8 * SIDE + q * 128, 128))
@@ -506,13 +608,7 @@
 
     every(0, depth * 8 // 256, 1, product)
 
-    row_id = lax.broadcasted_iota(jnp.int32, (8, rows), 0)
-
-    def edge_rows(ref, z, h):
-        line = get(ref.at[h], pl.ds(z, 1))
-        return jnp.where(row_id == 7 * h, line, 0.0)
-
-    def chain(i, below):
+    def chain(state, i, below):
         z = depth - 1 - i
         eight = pl.ds(pl.multiple_of(z * 8, 8), 8)
         solved = []
@@ -520,8 +616,9 @@
             at = pl.multiple_of(z * cols + 8 * h, 8)
             part = pl.ds(at, 8)
             across = get(fx, pl.ds(pl.multiple_of(at + 8, 8), 8)) - get(fx, pl.ds(at + 7, 8))
-            e = (part_exp[part, :] + across) + (src[h, eight, :] + edge_rows(edge_flux, z, h))
-            v = fac[part, :] * below[h] + rec[part, :] * e
+            e = (get(state, part) + flux_y[part, :]) + (across + src[h, eight, :])
+            e = e + edge_rows(edge_flux, z, h, rows)
+            v = below[h] + rec[part, :] * (e - below[h])
             put(low, part, v)
             solved.append(v)
         return tuple(solved)
@@ -535,7 +632,7 @@
 
     edges(0)
     nothing = (jnp.zeros((8, rows), jnp.float32),) * 2
-    lax.fori_loop(0, depth, chain, nothing, unroll=4)
+    lax.fori_loop(0, depth, functools.partial(chain, adj), nothing, unroll=4)
 
     def inc_copy(level, to):
         return pltpu.make_async_remote_copy(
@@ -558,13 +655,12 @@
             send_inc[level] = get(low, first) + get(dec, first) * recv_inc[level]
             inc_copy(level, gz - 1).start()
 
-    load_prs.wait()
     early = gz < n_gz // 2
 
     @pl.when(early)
     def _():
-        send_pressures()
-        face_terms(0, False)
+        face_terms(0, False, False)
+        every(0, depth, UNROLL, prepare_terms)
 
     relay(0)
 
@@ -597,15 +693,15 @@
         lateral(1, a, a_next, at, tx[here, :], ty[here, :])
 
     every(0, depth, UNROLL, level_second)
+    every(0, cells // block, 4, flux_steps)
 
     @pl.when(early)
     def _():
-        face_terms(1, True)
+        face_terms(1, True, True)
 
     @pl.when(jnp.logical_not(early))
     def _():
-        send_pressures()
-        face_terms(1, False)
+        face_terms(1, False, False)
 
     for s in range(2):
 
@@ -614,12 +710,12 @@
             mid_come(s).wait_recv()
 
     edges(1)
-    lax.fori_loop(0, depth, chain, nothing, unroll=4)
+    lax.fori_loop(0, depth, functools.partial(chain, mid), nothing, unroll=4)
     relay(1)
 
     @pl.when(jnp.logical_not(early))
     def _():
-        face_terms(0, True)
+        face_terms(0, True, False)
 
     for s in range(2):
 
@@ -629,17 +725,7 @@
 
     edge_terms()
 
-    def finish(z):
-        at = pl.multiple_of(z * cols, cols)
-        here = pl.ds(at, cols)
-        out_ref[here, :] = get(low, here) + get(dec, here) * recv_inc[1]
-        along = gy_sum[here, :]
-        along = along + pltpu.roll(along, 1, 1)
-        across = get(gx_sum, lower(at)) + get(gx_sum, pl.ds(at + 7, cols))
-        ends = jnp.concatenate([edge_rows(edge_term, z, h) for h in range(2)], axis=0)
-        grad_ref[here, :] = mobility(get(mob, here)) * ((along + across) + ends)
-
-    every(0, depth, 4, finish)
+    inc_ref[...] = recv_inc[1]
 
     for j in range(1, n_gz):
         surf_copy(j).wait_send()
@@ -682,11 +768,22 @@
     dma = pltpu.SemaphoreType.DMA
     wide = cols + 2 * HALF
     hbm = pl.BlockSpec(memory_space=pl.ANY)
-    adjoint_start, gradient = pl.pallas_call(
+    in_vmem = pl.BlockSpec(memory_space=vmem)
+    kept = (
+        banded,
+        banded,
+        vmem((cols, rows), f32),
+        banded,
+        field,
+        banded,
+        vmem((2, lanes, depth, LANES), f32),
+        vmem((cols, rows), f32),
+    )
+    state = pl.pallas_call(
         functools.partial(window_kernel, n_gx, n_gz, depth, cols, rows),
-        out_shape=(vmem((cells, rows), f32),) * 2,
+        out_shape=kept,
         in_specs=[hbm] * 9,
-        out_specs=(pl.BlockSpec(memory_space=vmem),) * 2,
+        out_specs=(in_vmem,) * len(kept),
         scratch_shapes=[
             vmem(residual.shape, f32),
             vmem(whitening.shape, f32),
@@ -699,15 +796,16 @@
             vmem((cells, rows), b16),
             field,
             field,
+            field,
             banded,
+            vmem((cells, rows), b16),
+            field,
+            vmem((2, cells, rows), f32),
             banded,
             field,
             field,
-            vmem((2, cells, rows), f32),
             field,
             field,
-            banded,
-            banded,
             banded,
             vmem((2, depth * 8, rows), f32),
             vmem((n_gz, wide, rows // n_gz), f32),
@@ -722,7 +820,8 @@
             vmem((2, 2, depth, rows), f32),
             vmem((2, depth, rows), f32),
             vmem((2, lanes, depth, LANES), f32),
-            vmem((2, lanes, depth, LANES), f32),
+            vmem((rows, rows // 2), b16),
+            vmem((rows, rows // 2), b16),
             vmem((2, 2 * depth, rows), b16),
             vmem((2, 2 * depth, rows), b16),
             vmem((2, 2 * depth, rows), b16),
@@ -740,7 +839,7 @@
         ]
         + [dma((2,))] * 12,
         compiler_params=pltpu.CompilerParams(
-            collective_id=0, has_side_effects=True, vmem_limit_bytes=56 * 1024 * 1024
+            collective_id=0, has_side_effects=True, vmem_limit_bytes=50 * 1024 * 1024
         ),
     )(
         residual,
@@ -753,6 +852,14 @@
         log_permeability.reshape(cells, rows),
         vertical.reshape(cells, rows),
     )
+    adjoint_start, gradient = pl.pallas_call(
+        functools.partial(finish_kernel, n_gx, depth, cols, rows),
+        out_shape=(jax.ShapeDtypeStruct((cells, rows), f32),) * 2,
+        in_specs=[in_vmem] * len(kept),
+        out_specs=(hbm, hbm),
+        scratch_shapes=[field, field, dma((STORES, 2))],
+        compiler_params=pltpu.CompilerParams(vmem_limit_bytes=8 * 1024 * 1024),
+    )(*state)
     shape = (depth, cols, rows)
     return adjoint_start.reshape(shape), gradient.reshape(shape)
 

time: 41 us -> 37.8 us (0.922); the launches traced: 40.4 us -> 37.7 us
  local copies, waits for them, and re-layouts: 2.64 us -> 0 us
    unnamed x2 -> x0, local copies, waits for them, and re-layouts: 2.64 us -> none
    pallas_call x1, Pallas kernels: 37.1 us -> 34.8 us  [on_device(): pl.pallas_call(functools.partial(window_kernel, n_gx, n_gz, depth, cols,...]
    pallas_call x0 -> x1, Pallas kernels: none -> 2.33 us  [on_device(): pl.pallas_call(functools.partial(finish_kernel, n_gx, depth, cols, rows),...]
where the time goes in v2:
time: 37.8 us; the launch traced here: 37.7 us
  Pallas kernels  37.1 us (98%)
  between operations  0.64 us (2%)
    pallas_call x1, Pallas kernels, on_device(): pl.pallas_call(functools.partial(window_kernel, n_gx, n_gz, depth, cols,...  34.8 us
    pallas_call x1, Pallas kernels, on_device(): pl.pallas_call(functools.partial(finish_kernel, n_gx, depth, cols, rows),...  2.33 us

profile of v2, /device:TPU:33, one launch (start us, length us, event | category | flops | bytes accessed | tf_op | source)
XLA Modules:
  0.0 37.7 jit_solution(10843535339300243658)
XLA Ops:
  0.6 34.8 %shard_map.104 = (f32[4,1032,128]{2,1,0:T(8,128)S(1)}, f32[4,1032,128]{2,1,0:T(8,128)S(1)}, f32[16,512]{1,0:T(8,128)S(1)}, f32[4,1032,128]{2,1,0:T(8,128)S(1)}, ...) custom-call(f32[16,128]{1,0:T(8,128)} %residual_hbm.1, ...), custom_call_target="tpu_custom_call" | custom-call | tf_op jit(solution)/shard_map/pallas_call | solution.py:782
  35.4 2.3 %shard_map.105 = (f32[1024,512]{1,0:T(8,128)}, f32[1024,512]{1,0:T(8,128)}) custom-call(f32[4,1032,128]{2,1,0:T(8,128)S(1)} %get-tuple-element.12.low, f32[4,1032,128]{2,1,0:T(8,128)S(1)} %get-tuple-element.13.dec, f32[16,512]{1,0:T(8,128)S(1)} %get-tuple-element.14.inc_ref, f32[4,1032,128]{2,1,0:T(8,128)S(1)} %get-tuple-element.15.gx_sum, ...), custom_call_target="tpu_custom_call" | custom-call | tf_op jit(solution)/shard_map/pallas_call | solution.py:855

commit v3 on v2

--- a/solution.py
+++ b/solution.py
@@ -12,9 +12,9 @@
 SIDE = 17
 FAR = 1e6
 MESH = pl.DeviceIdType.MESH
-CHUNKS = 2
+CHUNKS = 1
 UNROLL = 4
-STORES = 4
+STORES = 8
 SPLIT = 48
 LANES = 128
 
@@ -300,7 +300,7 @@
         toep_hi[tile, :] = hi
         toep_lo[tile, :] = (piece - hi.astype(jnp.float32)).astype(jnp.bfloat16)
 
-    every(0, depth * 8 // 64, 1, halve)
+    every(0, depth * 8 // 64, 4, halve)
 
     tile = rows // 2
     k_id = lax.broadcasted_iota(jnp.int32, (rows, tile), 0)
@@ -309,6 +309,30 @@
     pair_sum[...] = jnp.where(same, 1.0, jnp.where(nearby, 1.0, 0.0)).astype(jnp.bfloat16)
     same, nearby = k_id == n_id + tile, k_id + 1 == n_id + tile
     pair_step[...] = jnp.where(same, 1.0, jnp.where(nearby, -1.0, 0.0)).astype(jnp.bfloat16)
+
+    block = 16 * cols
+
+    def product_of(lhs, rhs):
+        return jnp.dot(lhs, rhs, preferred_element_type=jnp.float32)
+
+    def mobilities(i):
+        at = pl.ds(pl.multiple_of(i * block, block), block)
+        m = (0.5 * STEP_SIZE) * jnp.exp(get(logk, at))
+        put(mob, at, m)
+        m = m.astype(jnp.bfloat16)
+        face_y[at, :tile] = product_of(m, pair_sum[...])
+        face_y[at, tile:] = product_of(m[:, tile:], pair_sum[:tile, :])
+
+    def flux_steps(i):
+        at = pl.ds(pl.multiple_of(i * block, block), block)
+        f = fy_narrow[at, :]
+        flux_y[at, :tile] = product_of(f[:, :tile], pair_step[tile:, :])
+        flux_y[at, tile:] = product_of(f, pair_step[...])
+
+    for c in reversed(range(CHUNKS)):
+        for copy in chunk_loads[c][: 2 * bands]:
+            copy.wait()
+        every(c * span // block, (c + 1) * span // block, 4, mobilities)
 
     strips_beside = jnp.where(has[0], 1, 0) + jnp.where(has[1], 1, 0)
     pl.semaphore_wait(barrier, n_gz - 1 + strips_beside)
@@ -338,30 +362,6 @@
     for j in range(1, n_gz):
         surf_copy(j).start()
 
-    block = 16 * cols
-
-    def product_of(lhs, rhs):
-        return jnp.dot(lhs, rhs, preferred_element_type=jnp.float32)
-
-    def mobilities(i):
-        at = pl.ds(pl.multiple_of(i * block, block), block)
-        m = (0.5 * STEP_SIZE) * jnp.exp(get(logk, at))
-        put(mob, at, m)
-        m = m.astype(jnp.bfloat16)
-        face_y[at, :tile] = product_of(m, pair_sum[...])
-        face_y[at, tile:] = product_of(m[:, tile:], pair_sum[:tile, :])
-
-    def flux_steps(i):
-        at = pl.ds(pl.multiple_of(i * block, block), block)
-        f = fy_narrow[at, :]
-        flux_y[at, :tile] = product_of(f[:, :tile], pair_step[tile:, :])
-        flux_y[at, tile:] = product_of(f, pair_step[...])
-
-    for c in reversed(range(CHUNKS)):
-        for copy in chunk_loads[c][: 2 * bands]:
-            copy.wait()
-        every(c * span // block, (c + 1) * span // block, 2, mobilities)
-
     def pack(i):
         z0 = pl.multiple_of(i * 16, 16)
         r0 = pl.multiple_of(i * 16 * cols, 16 * cols)
@@ -373,7 +373,7 @@
             for k, field in enumerate(fields):
                 send_halo[s, pl.ds(k * depth + z0, 16), :] = field.astype(jnp.bfloat16)
 
-    every(0, depth // 16, 1, pack)
+    every(0, depth // 16, 2, pack)
 
     def swap(sent, arrived, send_sem, recv_sem):
         def leave(s):
@@ -498,7 +498,7 @@
                 far_m = recv_halo[s, pl.ds(pl.multiple_of(depth + i * 16, 16), 16), :]
                 put(edge_flux.at[s], part, (near_mob[s, part, :] + far_m.astype(jnp.float32)) * d)
 
-        every(0, depth // 16, 1, step)
+        every(0, depth // 16, 4, step)
 
     def edge_terms():
         def step(i):
@@ -512,7 +512,7 @@
                     total = term if total is None else total + term
                 put(edge_term.at[s], part, total)
 
-        every(0, depth // 16, 1, step)
+        every(0, depth // 16, 4, step)
 
     def pressure_steps(level, z, at):
         zf = (z_base + z).astype(jnp.float32)
@@ -606,7 +606,7 @@
                 + jnp.dot(toep_lo[tile, :], rhs_hi[h], preferred_element_type=jnp.float32)
             )
 
-    every(0, depth * 8 // 256, 1, product)
+    every(0, depth * 8 // 256, 2, product)
 
     def chain(state, i, below):
         z = depth - 1 - i
@@ -674,7 +674,7 @@
             near_adj[1, s, pl.ds(z0, 16), :] = value
             send_mid[s, pl.ds(z0, 16), :] = value.astype(jnp.bfloat16)
 
-    every(0, depth // 16, 2, pack_mid)
+    every(0, depth // 16, 4, pack_mid)
 
     for s in range(2):
 

time: 37.8 us -> 36.8 us (0.974)
  Pallas kernels: 37.1 us -> 36 us
    pallas_call x1, Pallas kernels: 34.8 us -> 33.8 us  [on_device(): pl.pallas_call(functools.partial(window_kernel, n_gx, n_gz, depth, cols,...]
where the time goes in v3:
time: 36.8 us; the launch traced here: 36.7 us
  Pallas kernels  36 us (98%)
  between operations  0.64 us (2%)
    pallas_call x1, Pallas kernels, on_device(): pl.pallas_call(functools.partial(window_kernel, n_gx, n_gz, depth, cols,...  33.8 us
    pallas_call x1, Pallas kernels, on_device(): pl.pallas_call(functools.partial(finish_kernel, n_gx, depth, cols, rows),...  2.26 us

profile of v3, /device:TPU:33, one launch (start us, length us, event | category | flops | bytes accessed | tf_op | source)
XLA Modules:
  0.0 36.7 jit_solution(5592779008615317445)
XLA Ops:
  0.6 33.8 %shard_map.104 = (f32[4,1032,128]{2,1,0:T(8,128)S(1)}, f32[4,1032,128]{2,1,0:T(8,128)S(1)}, f32[16,512]{1,0:T(8,128)S(1)}, f32[4,1032,128]{2,1,0:T(8,128)S(1)}, ...) custom-call(f32[16,128]{1,0:T(8,128)} %residual_hbm.1, ...), custom_call_target="tpu_custom_call" | custom-call | tf_op jit(solution)/shard_map/pallas_call | solution.py:782
  34.4 2.3 %shard_map.105 = (f32[1024,512]{1,0:T(8,128)}, f32[1024,512]{1,0:T(8,128)}) custom-call(f32[4,1032,128]{2,1,0:T(8,128)S(1)} %get-tuple-element.12.low, f32[4,1032,128]{2,1,0:T(8,128)S(1)} %get-tuple-element.13.dec, f32[16,512]{1,0:T(8,128)S(1)} %get-tuple-element.14.inc_ref, f32[4,1032,128]{2,1,0:T(8,128)S(1)} %get-tuple-element.15.gx_sum, ...), custom_call_target="tpu_custom_call" | custom-call | tf_op jit(solution)/shard_map/pallas_call | solution.py:855

commit v4 on v3

--- a/solution.py
+++ b/solution.py
@@ -83,7 +83,7 @@
 
     pending = []
     for c in range(STORES):
-        every(c * chunk, (c + 1) * chunk, 4, finish)
+        every(c * chunk, (c + 1) * chunk, 8, finish)
         copies = stores(c)
         for copy in copies:
             copy.start()
@@ -274,7 +274,7 @@
         return jnp.where(cell == wells_ref[i], FAR, top)
 
     top = lax.fori_loop(
-        0, wells_ref.shape[0], drill, top_ref[...].astype(jnp.float32), unroll=8
+        0, wells_ref.shape[0], drill, top_ref[...].astype(jnp.float32), unroll=16
     )
     x_id = lax.broadcasted_iota(jnp.int32, (cols, rows), 0)
     y_id = lax.broadcasted_iota(jnp.int32, (cols, rows), 1)
@@ -562,7 +562,7 @@
             send_prs[0, part, :] = lines[:16, :]
             send_prs[1, part, :] = lines[16:, :]
 
-        every(0, 2 * depth // 16, 1, step)
+        every(0, 2 * depth // 16, 4, step)
     load_prs.wait()
     pack_pressures()
 

time: 36.8 us -> 36.7 us (level)
  no operation moved by 1% of the time
where the time goes in v4:
time: 36.7 us; the launch traced here: 36.6 us
  Pallas kernels  35.9 us (98%)
  between operations  0.64 us (2%)
    pallas_call x1, Pallas kernels, on_device(): pl.pallas_call(functools.partial(window_kernel, n_gx, n_gz, depth, cols,...  33.8 us
    pallas_call x1, Pallas kernels, on_device(): pl.pallas_call(functools.partial(finish_kernel, n_gx, depth, cols, rows),...  2.18 us

profile of v4, /device:TPU:33, one launch (start us, length us, event | category | flops | bytes accessed | tf_op | source)
XLA Modules:
  0.0 36.6 jit_solution(2412572195344539895)
XLA Ops:
  0.6 33.8 %shard_map.104 = (f32[4,1032,128]{2,1,0:T(8,128)S(1)}, f32[4,1032,128]{2,1,0:T(8,128)S(1)}, f32[16,512]{1,0:T(8,128)S(1)}, f32[4,1032,128]{2,1,0:T(8,128)S(1)}, ...) custom-call(f32[16,128]{1,0:T(8,128)} %residual_hbm.1, ...), custom_call_target="tpu_custom_call" | custom-call | tf_op jit(solution)/shard_map/pallas_call | solution.py:782
  34.4 2.2 %shard_map.105 = (f32[1024,512]{1,0:T(8,128)}, f32[1024,512]{1,0:T(8,128)}) custom-call(f32[4,1032,128]{2,1,0:T(8,128)S(1)} %get-tuple-element.12.low, f32[4,1032,128]{2,1,0:T(8,128)S(1)} %get-tuple-element.13.dec, f32[16,512]{1,0:T(8,128)S(1)} %get-tuple-element.14.inc_ref, f32[4,1032,128]{2,1,0:T(8,128)S(1)} %get-tuple-element.15.gx_sum, ...), custom_call_target="tpu_custom_call" | custom-call | tf_op jit(solution)/shard_map/pallas_call | solution.py:855
